TPU v7x, 32 devices: a whole 2x2x4 slice. The times are simulated.
32 devices in a mesh: vec: 8 (over z, y), pair: 4 (over x, core).
Axes of the slice: x: 2, y: 2, z: 4, core: 2. Of those that a mesh axis runs over, the one named last changes fastest.
Arguments:
- green: bfloat16 [256, 32768], P('vec', 'pair'), may hold values from -6 to 6
- chol: bfloat16 [24576, 32768], P('vec', 'pair'), may hold values from -0.03125 to 0.03125
- fields: bfloat16 [256, 24576], P(None, 'vec'), may hold values from -5 to 5
Outputs:
- potential: float32 [256, 32768], P('vec', 'pair')
- log_weight: float32 [256], P('pair')
All inputs are finite; a program needn't handle non-finite values.
Results may differ from a plain program's by a relative error of at most 0.0026.
Values may be sent and summed in bfloat16 or wider, within the bound.
A program may use at most 128 MiB of HBM per device.

v0:
```python
import jax
import jax.numpy as jnp
from jax import lax
from jax.sharding import PartitionSpec as P

NCHOL = 24576


def shards(green, chol, fields):
    local_walk = green.shape[0]
    walkers = local_walk * lax.axis_size("vec")
    share = walkers // lax.axis_size("pair")
    first = lax.axis_index("pair") * share
    partial_force = lax.dot_general(
        lax.all_gather(green, "vec", axis=0, tiled=True),
        chol,
        (((1,), (1,)), ((), ())),
        preferred_element_type=jnp.float32,
    )
    own_fields = lax.dynamic_slice_in_dim(fields, first, share, 0).astype(jnp.float32)
    force = lax.psum(partial_force, "pair")
    bias = jnp.tanh(force)
    shifted = (fields.astype(jnp.float32) - bias).astype(jnp.bfloat16)
    own_bias = lax.dynamic_slice_in_dim(bias, first, share, 0)
    weight_terms = jnp.sum(own_fields * own_bias - 0.5 * own_bias * own_bias, axis=1) / NCHOL
    log_weight = lax.psum(weight_terms, "vec")
    potential = lax.psum_scatter(
        jnp.dot(shifted, chol, preferred_element_type=jnp.float32),
        "vec",
        scatter_dimension=0,
        tiled=True,
    )
    return (potential, log_weight)


def solution(mesh):
    return jax.shard_map(
        shards,
        mesh=mesh,
        in_specs=(P("vec", "pair"), P("vec", "pair"), P(None, "vec")),
        out_specs=(P("vec", "pair"), P("pair")),
        check_vma=False,
    )
```

profile of v0, /device:TPU:0, one launch (start us, length us, event | category | flops | bytes accessed | tf_op | source)
XLA Modules:
  0.0 357.0 jit_solution(16329099251398800466)
XLA Ops:
  7.2 0.0 all-gather.2.cloned.1.call-start
  7.2 0.7 all-gather.2.cloned.1.call-update
  7.9 0.0 all-reduce.2.cloned.1.call-start
  7.9 78.3 %all-gather.2.cloned.1.call-done = bf16[256,8192]{1,0:T(8,128)(2,1)} async-done(((bf16[32,8192]{1,0:T(8,128)(2,1)}), bf16[256,8192]{1,0:T(8,128)(2,1)}) %all-gather.2.cloned.1.call-update) | async-done | bytes 4194320 | tf_op jit(solution)/shard_map/all_gather | solution.py:15
  86.3 22.6 %fusion.4 = f32[256,3072]{1,0:T(8,128)} fusion(bf16[256,8192]{1,0:T(8,128)(2,1)} %all-gather.2.cloned.1.call-done, bf16[3072,8192]{1,0:T(8,128)(2,1)} %param.4), kind=kOutput, calls=%fused_computation.7 | convolution fusion | flops 12884901888 | bytes 57671680 | tf_op jit(solution)/shard_map/dot_general | solution.py:14
  108.8 0.0 copy-start.1
  108.8 0.0 all-reduce.2.cloned.1.call-update
  108.9 0.0 reduce-scatter.2.cloned.1.call-start
  108.9 66.8 %all-reduce.2.cloned.1.call-done = f32[256,3072]{1,0:T(8,128)} async-done(((f32[256,3072]{1,0:T(8,128)}), f32[256,3072]{1,0:T(8,128)}) %all-reduce.2.cloned.1.call-update) | async-done | bytes 3145744 | tf_op jit(solution)/shard_map/psum | solution.py:21
  175.7 0.0 copy-done.1
  175.7 25.2 %fusion = f32[256,8192]{1,0:T(8,128)} fusion(bf16[3072,8192]{1,0:T(8,128)(2,1)} %param.4, bf16[256,3072]{1,0:T(8,128)(2,1)S(1)} %copy-done.1, f32[256,3072]{1,0:T(8,128)} %all-reduce.2.cloned.1.call-done), kind=kOutput, calls=%fused_computation.1 | convolution fusion | flops 12887261184 | bytes 63438848 | tf_op jit(solution)/shard_map/dot_general | solution.py:28
  200.9 0.0 copy-start
  200.9 0.0 reduce-scatter.2.cloned.1.call-update
  201.0 1.9 copy-done
  202.8 0.4 tanh.3
  203.2 1.3 fusion.2
  204.5 22.9 %psum.15 = f32[64]{0:T(128)} all-reduce(f32[64]{0:T(128)S(1)} %broadcast_multiply_fusion), channel_id=1, replica_groups=mesh['vec'=8,'pair'=4] {'vec'}, use_global_device_ids=true, to_apply=%region_3.0 | all-reduce | flops 64 | bytes 512 | tf_op jit(solution)/shard_map/psum | solution.py:26
  227.4 123.1 %reduce-scatter.2.cloned.1.call-done = f32[32,8192]{1,0:T(8,128)} async-done(((f32[256,8192]{1,0:T(8,128)}), f32[32,8192]{1,0:T(8,128)}) %reduce-scatter.2.cloned.1.call-update) | async-done | bytes 1048592 | tf_op jit(solution)/shard_map/reduce_scatter | solution.py:27
  (1 shorter events, 0.0 us)
Async XLA Ops:
  7.2 79.1 %all-gather.2.cloned.1.call-start = ((), (), s32[]{:S(2)}) async-start(), calls=%async_computation.1 | async-start | bytes 4718592 | tf_op jit(solution)/shard_map/all_gather | solution.py:15
  7.9 167.8 %all-reduce.2.cloned.1.call-start = ((), (), s32[]{:S(2)}) async-start(), calls=%async_computation.2 | async-start | bytes 6291456 | tf_op jit(solution)/shard_map/psum | solution.py:21
  108.8 66.9 %copy-start.1 = (bf16[256,3072]{1,0:T(8,128)(2,1)S(1)}, bf16[256,3072]{1,0:T(8,128)(2,1)}, u32[]{:S(2)}) copy-start(bf16[256,3072]{1,0:T(8,128)(2,1)} %param.5) | copy-start | bytes 4718596
  108.9 241.7 %reduce-scatter.2.cloned.1.call-start = ((), (), s32[]{:S(2)}) async-start(), calls=%async_computation.3 | async-start | bytes 9437184 | tf_op jit(solution)/shard_map/reduce_scatter | solution.py:27
  200.9 1.9 copy-start
Sparse Core Ops, SparseCore 0:
  10.1 76.0 all-gather.1
  109.0 66.6 all-reduce.1
  201.1 149.3 reduce-scatter.1
where the time goes:
time: 357 us
  waiting for transfers between devices  269 us (75%)
  matrix products  47.8 us (13%)
  blocking collectives  22.9 us (6%)
  between operations  13.8 us (4%)
    reduce_scatter x1, waiting for transfers between devices, shards(): lax.psum_scatter(jnp.dot(shifted, chol, preferred_element_type=jnp.float3...  123 us
    all_gather x1, waiting for transfers between devices, shards(): lax.all_gather(green, 'vec', axis=0, tiled=True)  78.3 us
    psum x1, waiting for transfers between devices, shards(): force = lax.psum(partial_force, 'pair')  66.8 us
    dot_general x1, matrix products, shards(): jnp.dot(shifted, chol, preferred_element_type=jnp.float32)  25.2 us
    psum x1, blocking collectives, shards(): log_weight = lax.psum(weight_terms, 'vec')  22.9 us
    dot_general x1, matrix products, shards(): lax.dot_general(lax.all_gather(green, 'vec', axis=0, tiled=True), chol, (...  22.6 us
  transfers between devices with their start and end apart: 3, of which 3 were waited for; matrix products, arithmetic and copies ran while one was open for 0% of the time, Pallas kernels for 0%

commit v1 on v0

v1 whole, which is shorter than its diff:
```python
import functools

import jax
import jax.numpy as jnp
from jax import lax
from jax.experimental import pallas as pl
from jax.experimental.pallas import tpu as pltpu
from jax.sharding import PartitionSpec as P

MESH = pl.DeviceIdType.MESH
LAG = 4
BUFS = 3


def kernel(
    dims,
    green_ref, chol_ref, fields_ref, out_ref, lw_ref,
    G, F, r1, s2, r2, SH, fbuf, acc, cb1, cb2, tmp, yS, yR, keep, zS, zR, lw_in,
    c1_sem, c2_sem, f_sem,
    gz_s, gz_r, gy_s, gy_r, e1_s, e1_r, e2_s, e2_r, e3_s, e3_r, e4_s, e4_r,
    py_s, py_r, pz_s, pz_r, lw_s, lw_r,
):
    V, Z, NP, X, LW, S, C, K, NK, KB, NC, CB, NB, TN = dims
    W = V * LW
    v = lax.axis_index("vec")
    p = lax.axis_index("pair")
    z, y = v // 2, v % 2
    x, q = p // 2, p % 2
    y_peer = (z * 2 + 1 - y, p)
    core_peer = (v, x * 2 + 1 - q)

    def z_at(d):
        return lax.rem(z + d, Z)

    def x_at(d):
        return lax.rem(x + d, X)

    def remote(src, dst, send, recv, to):
        return pltpu.make_async_remote_copy(
            src_ref=src, dst_ref=dst, send_sem=send, recv_sem=recv, device_id=to, device_id_type=MESH
        )

    def chol1(i):
        k, c = i // NC, i % NC
        rows = pl.ds(pl.multiple_of(c * CB, CB), CB)
        cols = pl.ds(pl.multiple_of(k * KB, KB), KB)
        slot = i % BUFS
        return pltpu.make_async_copy(chol_ref.at[rows, cols], cb1.at[slot], c1_sem.at[slot])

    def chol2(b):
        cols = pl.ds(pl.multiple_of(b * TN, TN), TN)
        slot = b % 2
        return pltpu.make_async_copy(chol_ref.at[:, cols], cb2.at[slot], c2_sem.at[slot])

    for i in range(BUFS - 1):
        chol1(i).start()
    chol2(0).start()
    own_rows = pl.ds(pl.multiple_of(p * S, S), S)
    load_fields = pltpu.make_async_copy(fields_ref.at[own_rows, :], fbuf, f_sem)
    load_fields.start()
    for k in range(NK):
        G[k, v] = green_ref[:, k * KB:(k + 1) * KB]

    barrier = pltpu.get_barrier_semaphore()
    for d in range(1, V):
        pl.semaphore_signal(barrier, inc=1, device_id=(lax.rem(v + d, V), p), device_id_type=MESH)
    pl.semaphore_signal(barrier, inc=1, device_id=core_peer, device_id_type=MESH)
    for d in range(1, X):
        pl.semaphore_signal(barrier, inc=1, device_id=(v, x_at(d) * 2 + q), device_id_type=MESH)
    pl.semaphore_wait(barrier, V - 1 + X)

    def gather_z(k, d):
        return remote(G.at[k, v], G.at[k, v], gz_s.at[k, d - 1], gz_r.at[k, d - 1], (z_at(d) * 2 + y, p))

    def gather_z_in(k, d):
        at = G.at[k, z_at(Z - d) * 2 + y]
        return remote(at, at, gz_s.at[k, d - 1], gz_r.at[k, d - 1], y_peer)

    def gather_y(k, d):
        at = G.at[k, z_at(Z - d) * 2 + y]
        return remote(at, at, gy_s.at[k, d], gy_r.at[k, d], y_peer)

    def gather_y_in(k, d):
        at = G.at[k, z_at(Z - d) * 2 + 1 - y]
        return remote(at, at, gy_s.at[k, d], gy_r.at[k, d], y_peer)

    def start_gather(k, carry):
        for d in range(1, Z):
            gather_z(k, d).start()
        gather_y(k, 0).start()
        return carry

    lax.fori_loop(0, NK, start_gather, 0)
    F[...] = jnp.zeros_like(F)
    acc[...] = jnp.zeros_like(acc)

    def forward(k):
        for d in range(1, Z):
            gather_z_in(k, d).wait_recv()
            gather_y(k, d).start()

    forward(0)

    def reduce_core(c):
        return remote(F.at[c, 1 - q], r1.at[c], e1_s.at[c], e1_r.at[c], core_peer)

    def force_step(i, carry):
        k, c = i // NC, i % NC

        @pl.when(c == 0)
        def _():
            @pl.when(k < NK - 1)
            def _():
                forward(k + 1)

            for d in range(Z):
                gather_y_in(k, d).wait_recv()

        @pl.when(i + BUFS - 1 < NK * NC)
        def _():
            chol1(i + BUFS - 1).start()

        chol1(i).wait()
        part = lax.dot_general(
            G[k].reshape(W, KB), cb1[i % BUFS], (((1,), (1,)), ((), ())), preferred_element_type=jnp.float32
        ).reshape(X, 2, S, CB)
        for h in range(2):
            F[c, h] += part[:, h]

        @pl.when(k == NK - 1)
        def _():
            reduce_core(c).start()

        return carry

    lax.fori_loop(0, NK * NC, force_step, 0)
    load_fields.wait()

    def reduce_x(c, d):
        return remote(s2.at[c, d - 1], r2.at[c, d - 1], e2_s.at[c, d - 1], e2_r.at[c, d - 1], (v, x_at(d) * 2 + q))

    def sum_cores(c, carry):
        reduce_core(c).wait_recv()
        for d in range(1, X):
            s2[c, d - 1] = F[c, q, x_at(d)] + r1[c, x_at(d)]
            reduce_x(c, d).start()
        return carry

    lax.fori_loop(0, NC, sum_cores, 0)

    def share_x(c, d):
        at = SH.at[c, p]
        return remote(at, at, e3_s.at[c, d - 1], e3_r.at[c, d - 1], (v, x_at(d) * 2 + q))

    def share_x_in(c, d):
        at = SH.at[c, x_at(X - d) * 2 + q]
        return remote(at, at, e3_s.at[c, d - 1], e3_r.at[c, d - 1], core_peer)

    def share_core(c, d):
        at = SH.at[c, x_at(X - d) * 2 + q]
        return remote(at, at, e4_s.at[c, d], e4_r.at[c, d], core_peer)

    def share_core_in(c, d):
        at = SH.at[c, x_at(X - d) * 2 + 1 - q]
        return remote(at, at, e4_s.at[c, d], e4_r.at[c, d], core_peer)

    def shift(c, carry):
        total = F[c, q, x] + r1[c, x]
        for d in range(1, X):
            reduce_x(c, d).wait_recv()
            total += r2[c, d - 1]
        bias = jnp.tanh(total)
        field = fbuf[:, pl.ds(pl.multiple_of(c * CB, CB), CB)].astype(jnp.float32)
        SH[c, p] = (field - bias).astype(jnp.bfloat16)
        for d in range(1, X):
            share_x(c, d).start()
        share_core(c, 0).start()
        terms = field * bias - 0.5 * bias * bias
        add = terms[:, :128]
        for j in range(1, CB // 128):
            add += terms[:, j * 128:(j + 1) * 128]
        acc[:S, :] += add
        return carry

    lax.fori_loop(0, NC, shift, 0)

    lw_in[0] = lax.dot_general(
        jnp.ones((8, 128), jnp.float32), acc[...], (((1,), (1,)), ((), ())),
        precision=lax.Precision.HIGHEST, preferred_element_type=jnp.float32,
    )

    def share_weight(d):
        return remote(lw_in.at[0], lw_in.at[d], lw_s.at[d - 1], lw_r.at[d - 1], (lax.rem(v + d, V), p))

    for d in range(1, V):
        share_weight(d).start()

    def pass_core(c, carry):
        for d in range(1, X):
            share_x_in(c, d).wait_recv()
            share_core(c, d).start()
        return carry

    lax.fori_loop(0, NC, pass_core, 0)

    def take_core(c, carry):
        for d in range(X):
            share_core_in(c, d).wait_recv()
        return carry

    lax.fori_loop(0, NC, take_core, 0)

    def scatter_y(b):
        return remote(yS.at[b], yR.at[b], py_s.at[b], py_r.at[b], y_peer)

    def scatter_z(b, d):
        return remote(zS.at[b, d - 1], zR.at[b, d - 1], pz_s.at[b, d - 1], pz_r.at[b, d - 1], (z_at(d) * 2 + y, p))

    def potential_step(b, carry):
        @pl.when(b < NB)
        def _():
            @pl.when(b + 1 < NB)
            def _():
                chol2(b + 1).start()

            chol2(b).wait()
            slot = b % 2
            total = jnp.zeros((W, TN), jnp.float32)
            for c in range(NC):
                total += jnp.dot(
                    SH[c].reshape(W, CB), cb2[slot, c * CB:(c + 1) * CB, :], preferred_element_type=jnp.float32
                )
            tmp[...] = total.reshape(Z, 2, LW, TN)
            yS[b] = tmp[:, 1 - y].astype(jnp.bfloat16)
            scatter_y(b).start()
            keep[b] = tmp[:, y]

        @pl.when(b >= LAG)
        def _():
            e = b - LAG
            scatter_y(e).wait_recv()
            for d in range(1, Z):
                zS[e, d - 1] = (keep[e, z_at(d)] + yR[e, z_at(d)].astype(jnp.float32)).astype(jnp.bfloat16)
                scatter_z(e, d).start()

        return carry

    lax.fori_loop(0, NB + LAG, potential_step, 0)

    def finish(b, carry):
        total = keep[b, z] + yR[b, z].astype(jnp.float32)
        for d in range(1, Z):
            scatter_z(b, d).wait_recv()
            total += zR[b, d - 1].astype(jnp.float32)
        out_ref[:, pl.ds(pl.multiple_of(b * TN, TN), TN)] = total
        return carry

    lax.fori_loop(0, NB, finish, 0)

    weight = lw_in[0]
    for d in range(1, V):
        share_weight(d).wait_recv()
        weight += lw_in[d]
        share_weight(d).wait_send()
    lw_ref[...] = weight

    def sent_gather(k, carry):
        for d in range(1, Z):
            gather_z(k, d).wait_send()
        for d in range(Z):
            gather_y(k, d).wait_send()
        return carry

    lax.fori_loop(0, NK, sent_gather, 0)

    def sent_share(c, carry):
        reduce_core(c).wait_send()
        for d in range(1, X):
            reduce_x(c, d).wait_send()
            share_x(c, d).wait_send()
        for d in range(X):
            share_core(c, d).wait_send()
        return carry

    lax.fori_loop(0, NC, sent_share, 0)

    def sent_scatter(b, carry):
        scatter_y(b).wait_send()
        for d in range(1, Z):
            scatter_z(b, d).wait_send()
        return carry

    lax.fori_loop(0, NB, sent_scatter, 0)


def shards(green, chol, fields):
    V, NP = lax.axis_size("vec"), lax.axis_size("pair")
    Z, X = V // 2, NP // 2
    LW, K = green.shape
    C = chol.shape[0]
    W = V * LW
    S = W // NP
    NK = 8
    KB = K // NK
    CB = 512
    NC = C // CB
    TN = 512
    NB = K // TN
    dims = (V, Z, NP, X, LW, S, C, K, NK, KB, NC, CB, NB, TN)
    bf, f32 = jnp.bfloat16, jnp.float32
    dma = pltpu.SemaphoreType.DMA
    potential, weight = pl.pallas_call(
        functools.partial(kernel, dims),
        out_shape=(jax.ShapeDtypeStruct((LW, K), f32), jax.ShapeDtypeStruct((8, 128), f32)),
        in_specs=[
            pl.BlockSpec(memory_space=pltpu.VMEM),
            pl.BlockSpec(memory_space=pl.ANY),
            pl.BlockSpec(memory_space=pl.ANY),
        ],
        out_specs=(pl.BlockSpec(memory_space=pltpu.VMEM), pl.BlockSpec(memory_space=pltpu.VMEM)),
        scratch_shapes=[
            pltpu.VMEM((NK, V, LW, KB), bf),
            pltpu.VMEM((NC, 2, X, S, CB), f32),
            pltpu.VMEM((NC, X, S, CB), f32),
            pltpu.VMEM((NC, X - 1, S, CB), f32),
            pltpu.VMEM((NC, X - 1, S, CB), f32),
            pltpu.VMEM((NC, NP, S, CB), bf),
            pltpu.VMEM((S, C), bf),
            pltpu.VMEM((128, 128), f32),
            pltpu.VMEM((BUFS, CB, KB), bf),
            pltpu.VMEM((2, C, TN), bf),
            pltpu.VMEM((Z, 2, LW, TN), f32),
            pltpu.VMEM((NB, Z, LW, TN), bf),
            pltpu.VMEM((NB, Z, LW, TN), bf),
            pltpu.VMEM((NB, Z, LW, TN), f32),
            pltpu.VMEM((NB, Z - 1, LW, TN), bf),
            pltpu.VMEM((NB, Z - 1, LW, TN), bf),
            pltpu.VMEM((V, 8, 128), f32),
            dma((BUFS,)), dma((2,)), dma(()),
            dma((NK, Z - 1)), dma((NK, Z - 1)), dma((NK, Z)), dma((NK, Z)),
            dma((NC,)), dma((NC,)), dma((NC, X - 1)), dma((NC, X - 1)),
            dma((NC, X - 1)), dma((NC, X - 1)), dma((NC, X)), dma((NC, X)),
            dma((NB,)), dma((NB,)), dma((NB, Z - 1)), dma((NB, Z - 1)),
            dma((V - 1,)), dma((V - 1,)),
        ],
        compiler_params=pltpu.CompilerParams(
            collective_id=0, has_side_effects=True, vmem_limit_bytes=56 * 1024 * 1024
        ),
        name="walker_step",
    )(green, chol, fields)
    return potential, weight[0, :S] / (C * V)


def solution(mesh):
    return jax.shard_map(
        shards,
        mesh=mesh,
        in_specs=(P("vec", "pair"), P("vec", "pair"), P(None, "vec")),
        out_specs=(P("vec", "pair"), P("pair")),
        check_vma=False,
    )
```

time: 357 us -> 157 us (0.44)
  waiting for transfers between devices: 269 us -> 0 us
  Pallas kernels: 0 us -> 152 us
  matrix products: 47.8 us -> 0 us
  blocking collectives: 22.9 us -> 0 us
  between operations: 13.8 us -> 0.64 us
    pallas_call x0 -> x1, Pallas kernels: none -> 152 us  [shards(): pl.pallas_call(functools.partial(kernel, dims), out_shape=(jax.ShapeDtype...]
    reduce_scatter x1 -> x0, waiting for transfers between devices: 123 us -> none  [shards(): lax.psum_scatter(jnp.dot(shifted, chol, preferred_element_type=jnp.float3...]
    all_gather x1 -> x0, waiting for transfers between devices: 78.3 us -> none  [shards(): lax.all_gather(green, 'vec', axis=0, tiled=True)]
    psum x1 -> x0, waiting for transfers between devices: 66.8 us -> none  [shards(): force = lax.psum(partial_force, 'pair')]
    dot_general x2 -> x0, matrix products: 47.8 us -> none  [the longest x1 25.2 us: shards(): jnp.dot(shifted, chol, preferred_element_type=jnp.float32)]
    psum x1 -> x0, blocking collectives: 22.9 us -> none  [shards(): log_weight = lax.psum(weight_terms, 'vec')]
  transfers between devices with their start and end apart: 3 -> 0, of which waited for: 3 -> 0; matrix products, arithmetic and copies ran while one was open for 0% -> 0% of each run, Pallas kernels for 0% -> 0%
where the time goes in v1:
time: 157 us; the launch traced here: 156 us
  Pallas kernels  152 us (97%)
  local copies, waits for them, and re-layouts  2.26 us (1%)
    pallas_call x1, Pallas kernels, shards(): pl.pallas_call(functools.partial(kernel, dims), out_shape=(jax.ShapeDtype...  152 us

profile of v1, /device:TPU:0, one launch (start us, length us, event | category | flops | bytes accessed | tf_op | source)
XLA Modules:
  0.0 156.3 jit_solution(13823762371408212686)
XLA Ops:
  0.6 152.2 %walker_step.1 = (f32[32,8192]{1,0:T(8,128)}, f32[8,128]{1,0:T(8,128)}) custom-call(bf16[32,8192]{1,0:T(8,128)(2,1)} %green_ref.1, bf16[3072,8192]{1,0:T(8,128)(2,1)} %chol_ref.1, bf16[256,3072]{1,0:T(8,128)(2,1)} %fields_ref.1), custom_call_target="tpu_custom_call" | custom-call | tf_op jit(solution)/shard_map/walker_step/pallas_call | solution.py:312
  152.9 1.2 multiply_bitcast_fusion
  154.1 2.3 %copy.6 = f32[32,8192]{1,0:T(8,128)} copy(f32[32,8192]{1,0:T(8,128)} %get-tuple-element.8) | data formatting | bytes 2097152

commit v2 on v1

--- a/solution.py
+++ b/solution.py
@@ -9,7 +9,8 @@
 
 MESH = pl.DeviceIdType.MESH
 LAG = 4
-BUFS = 3
+BUFS = 4
+AHEAD = 3
 
 
 def kernel(
@@ -21,7 +22,7 @@
     py_s, py_r, pz_s, pz_r, lw_s, lw_r,
 ):
     V, Z, NP, X, LW, S, C, K, NK, KB, NC, CB, NB, TN = dims
-    W = V * LW
+    HL, W2, S2, VS = LW // 2, V * LW // 2, S // 2, S // LW
     v = lax.axis_index("vec")
     p = lax.axis_index("pair")
     z, y = v // 2, v % 2
@@ -41,25 +42,25 @@
         )
 
     def chol1(i):
-        k, c = i // NC, i % NC
+        k, c = i // NC % NK, i % NC
         rows = pl.ds(pl.multiple_of(c * CB, CB), CB)
         cols = pl.ds(pl.multiple_of(k * KB, KB), KB)
         slot = i % BUFS
         return pltpu.make_async_copy(chol_ref.at[rows, cols], cb1.at[slot], c1_sem.at[slot])
 
-    def chol2(b):
-        cols = pl.ds(pl.multiple_of(b * TN, TN), TN)
-        slot = b % 2
+    def chol2(t):
+        cols = pl.ds(pl.multiple_of(t % NB * TN, TN), TN)
+        slot = t % 2
         return pltpu.make_async_copy(chol_ref.at[:, cols], cb2.at[slot], c2_sem.at[slot])
 
     for i in range(BUFS - 1):
         chol1(i).start()
     chol2(0).start()
-    own_rows = pl.ds(pl.multiple_of(p * S, S), S)
-    load_fields = pltpu.make_async_copy(fields_ref.at[own_rows, :], fbuf, f_sem)
+    load_fields = pltpu.make_async_copy(fields_ref.at[pl.ds(p * VS, VS)], fbuf, f_sem)
     load_fields.start()
-    for k in range(NK):
-        G[k, v] = green_ref[:, k * KB:(k + 1) * KB]
+    for h in range(2):
+        for k in range(NK):
+            G[h * NK + k, v] = green_ref[h * HL:(h + 1) * HL, k * KB:(k + 1) * KB]
 
     barrier = pltpu.get_barrier_semaphore()
     for d in range(1, V):
@@ -90,7 +91,7 @@
         gather_y(k, 0).start()
         return carry
 
-    lax.fori_loop(0, NK, start_gather, 0)
+    lax.fori_loop(0, AHEAD, start_gather, 0)
     F[...] = jnp.zeros_like(F)
     acc[...] = jnp.zeros_like(acc)
 
@@ -104,38 +105,6 @@
     def reduce_core(c):
         return remote(F.at[c, 1 - q], r1.at[c], e1_s.at[c], e1_r.at[c], core_peer)
 
-    def force_step(i, carry):
-        k, c = i // NC, i % NC
-
-        @pl.when(c == 0)
-        def _():
-            @pl.when(k < NK - 1)
-            def _():
-                forward(k + 1)
-
-            for d in range(Z):
-                gather_y_in(k, d).wait_recv()
-
-        @pl.when(i + BUFS - 1 < NK * NC)
-        def _():
-            chol1(i + BUFS - 1).start()
-
-        chol1(i).wait()
-        part = lax.dot_general(
-            G[k].reshape(W, KB), cb1[i % BUFS], (((1,), (1,)), ((), ())), preferred_element_type=jnp.float32
-        ).reshape(X, 2, S, CB)
-        for h in range(2):
-            F[c, h] += part[:, h]
-
-        @pl.when(k == NK - 1)
-        def _():
-            reduce_core(c).start()
-
-        return carry
-
-    lax.fori_loop(0, NK * NC, force_step, 0)
-    load_fields.wait()
-
     def reduce_x(c, d):
         return remote(s2.at[c, d - 1], r2.at[c, d - 1], e2_s.at[c, d - 1], e2_r.at[c, d - 1], (v, x_at(d) * 2 + q))
 
@@ -145,8 +114,6 @@
             s2[c, d - 1] = F[c, q, x_at(d)] + r1[c, x_at(d)]
             reduce_x(c, d).start()
         return carry
-
-    lax.fori_loop(0, NC, sum_cores, 0)
 
     def share_x(c, d):
         at = SH.at[c, p]
@@ -165,12 +132,14 @@
         return remote(at, at, e4_s.at[c, d], e4_r.at[c, d], core_peer)
 
     def shift(c, carry):
+        h = c // NC
         total = F[c, q, x] + r1[c, x]
         for d in range(1, X):
             reduce_x(c, d).wait_recv()
             total += r2[c, d - 1]
         bias = jnp.tanh(total)
-        field = fbuf[:, pl.ds(pl.multiple_of(c * CB, CB), CB)].astype(jnp.float32)
+        cols = pl.ds(pl.multiple_of(c % NC * CB, CB), CB)
+        field = fbuf[:, h, :, cols].reshape(S2, CB).astype(jnp.float32)
         SH[c, p] = (field - bias).astype(jnp.bfloat16)
         for d in range(1, X):
             share_x(c, d).start()
@@ -179,36 +148,73 @@
         add = terms[:, :128]
         for j in range(1, CB // 128):
             add += terms[:, j * 128:(j + 1) * 128]
-        acc[:S, :] += add
-        return carry
-
-    lax.fori_loop(0, NC, shift, 0)
-
-    lw_in[0] = lax.dot_general(
-        jnp.ones((8, 128), jnp.float32), acc[...], (((1,), (1,)), ((), ())),
-        precision=lax.Precision.HIGHEST, preferred_element_type=jnp.float32,
-    )
+        acc[:VS, h] += add.reshape(VS, HL, 128)
+        return carry
 
     def share_weight(d):
         return remote(lw_in.at[0], lw_in.at[d], lw_s.at[d - 1], lw_r.at[d - 1], (lax.rem(v + d, V), p))
 
-    for d in range(1, V):
-        share_weight(d).start()
-
     def pass_core(c, carry):
         for d in range(1, X):
             share_x_in(c, d).wait_recv()
             share_core(c, d).start()
         return carry
-
-    lax.fori_loop(0, NC, pass_core, 0)
 
     def take_core(c, carry):
         for d in range(X):
             share_core_in(c, d).wait_recv()
         return carry
 
-    lax.fori_loop(0, NC, take_core, 0)
+    def send_weight():
+        lw_in[0] = lax.dot_general(
+            jnp.ones((8, 128), jnp.float32), acc[...].reshape(128, 128), (((1,), (1,)), ((), ())),
+            precision=lax.Precision.HIGHEST, preferred_element_type=jnp.float32,
+        )
+        for d in range(1, V):
+            share_weight(d).start()
+
+    def force_step(i, carry):
+        k, c = i // NC, i % NC
+
+        @pl.when(c == 0)
+        def _():
+            @pl.when(k < 2 * NK - 1)
+            def _():
+                forward(k + 1)
+
+            @pl.when(k + AHEAD < 2 * NK)
+            def _():
+                start_gather(k + AHEAD, 0)
+
+            for d in range(Z):
+                gather_y_in(k, d).wait_recv()
+
+        @pl.when(i + BUFS - 1 < 2 * NK * NC)
+        def _():
+            chol1(i + BUFS - 1).start()
+
+        chol1(i).wait()
+        part = lax.dot_general(
+            G[k].reshape(W2, KB), cb1[i % BUFS], (((1,), (1,)), ((), ())), preferred_element_type=jnp.float32
+        ).reshape(X, 2, S2, CB)
+        e = k // NK * NC + c
+        for h in range(2):
+            F[e, h] += part[:, h]
+
+        @pl.when(k % NK == NK - 1)
+        def _():
+            reduce_core(e).start()
+
+        for at, stage in enumerate((sum_cores, shift, pass_core, take_core)):
+            @pl.when(k == NK + at)
+            def _():
+                stage(c, 0)
+
+        return carry
+
+    load_fields.wait()
+    lax.fori_loop(0, 2 * NK * NC, force_step, 0)
+    lax.fori_loop(NC, 2 * NC, sum_cores, 0)
 
     def scatter_y(b):
         return remote(yS.at[b], yR.at[b], py_s.at[b], py_r.at[b], y_peer)
@@ -217,20 +223,34 @@
         return remote(zS.at[b, d - 1], zR.at[b, d - 1], pz_s.at[b, d - 1], pz_r.at[b, d - 1], (z_at(d) * 2 + y, p))
 
     def potential_step(b, carry):
-        @pl.when(b < NB)
-        def _():
-            @pl.when(b + 1 < NB)
+        @pl.when(b == NB * 3 // 8)
+        def _():
+            lax.fori_loop(NC, 2 * NC, shift, 0)
+
+        @pl.when(b == NB * 6 // 8)
+        def _():
+            lax.fori_loop(NC, 2 * NC, pass_core, 0)
+            send_weight()
+
+        @pl.when(b == NB)
+        def _():
+            lax.fori_loop(NC, 2 * NC, take_core, 0)
+
+        @pl.when(b < 2 * NB)
+        def _():
+            @pl.when(b + 1 < 2 * NB)
             def _():
                 chol2(b + 1).start()
 
             chol2(b).wait()
             slot = b % 2
-            total = jnp.zeros((W, TN), jnp.float32)
+            total = jnp.zeros((W2, TN), jnp.float32)
             for c in range(NC):
                 total += jnp.dot(
-                    SH[c].reshape(W, CB), cb2[slot, c * CB:(c + 1) * CB, :], preferred_element_type=jnp.float32
+                    SH[b // NB * NC + c].reshape(W2, CB), cb2[slot, c * CB:(c + 1) * CB, :],
+                    preferred_element_type=jnp.float32,
                 )
-            tmp[...] = total.reshape(Z, 2, LW, TN)
+            tmp[...] = total.reshape(Z, 2, HL, TN)
             yS[b] = tmp[:, 1 - y].astype(jnp.bfloat16)
             scatter_y(b).start()
             keep[b] = tmp[:, y]
@@ -245,17 +265,18 @@
 
         return carry
 
-    lax.fori_loop(0, NB + LAG, potential_step, 0)
+    lax.fori_loop(0, 2 * NB + LAG, potential_step, 0)
 
     def finish(b, carry):
         total = keep[b, z] + yR[b, z].astype(jnp.float32)
         for d in range(1, Z):
             scatter_z(b, d).wait_recv()
             total += zR[b, d - 1].astype(jnp.float32)
-        out_ref[:, pl.ds(pl.multiple_of(b * TN, TN), TN)] = total
-        return carry
-
-    lax.fori_loop(0, NB, finish, 0)
+        rows = pl.ds(pl.multiple_of(b // NB * HL, HL), HL)
+        out_ref[rows, pl.ds(pl.multiple_of(b % NB * TN, TN), TN)] = total
+        return carry
+
+    lax.fori_loop(0, 2 * NB, finish, 0)
 
     weight = lw_in[0]
     for d in range(1, V):
@@ -271,7 +292,7 @@
             gather_y(k, d).wait_send()
         return carry
 
-    lax.fori_loop(0, NK, sent_gather, 0)
+    lax.fori_loop(0, 2 * NK, sent_gather, 0)
 
     def sent_share(c, carry):
         reduce_core(c).wait_send()
@@ -282,7 +303,7 @@
             share_core(c, d).wait_send()
         return carry
 
-    lax.fori_loop(0, NC, sent_share, 0)
+    lax.fori_loop(0, 2 * NC, sent_share, 0)
 
     def sent_scatter(b, carry):
         scatter_y(b).wait_send()
@@ -290,7 +311,7 @@
             scatter_z(b, d).wait_send()
         return carry
 
-    lax.fori_loop(0, NB, sent_scatter, 0)
+    lax.fori_loop(0, 2 * NB, sent_scatter, 0)
 
 
 def shards(green, chol, fields):
@@ -300,11 +321,12 @@
     C = chol.shape[0]
     W = V * LW
     S = W // NP
-    NK = 8
+    HL, S2 = LW // 2, S // 2
+    NK = 4
     KB = K // NK
     CB = 512
     NC = C // CB
-    TN = 512
+    TN = 1024
     NB = K // TN
     dims = (V, Z, NP, X, LW, S, C, K, NK, KB, NC, CB, NB, TN)
     bf, f32 = jnp.bfloat16, jnp.float32
@@ -319,35 +341,35 @@
         ],
         out_specs=(pl.BlockSpec(memory_space=pltpu.VMEM), pl.BlockSpec(memory_space=pltpu.VMEM)),
         scratch_shapes=[
-            pltpu.VMEM((NK, V, LW, KB), bf),
-            pltpu.VMEM((NC, 2, X, S, CB), f32),
-            pltpu.VMEM((NC, X, S, CB), f32),
-            pltpu.VMEM((NC, X - 1, S, CB), f32),
-            pltpu.VMEM((NC, X - 1, S, CB), f32),
-            pltpu.VMEM((NC, NP, S, CB), bf),
-            pltpu.VMEM((S, C), bf),
-            pltpu.VMEM((128, 128), f32),
+            pltpu.VMEM((2 * NK, V, HL, KB), bf),
+            pltpu.VMEM((2 * NC, 2, X, S2, CB), f32),
+            pltpu.VMEM((2 * NC, X, S2, CB), f32),
+            pltpu.VMEM((2 * NC, X - 1, S2, CB), f32),
+            pltpu.VMEM((2 * NC, X - 1, S2, CB), f32),
+            pltpu.VMEM((2 * NC, NP, S2, CB), bf),
+            pltpu.VMEM((S // LW, 2, HL, C), bf),
+            pltpu.VMEM((128 // LW, 2, HL, 128), f32),
             pltpu.VMEM((BUFS, CB, KB), bf),
             pltpu.VMEM((2, C, TN), bf),
-            pltpu.VMEM((Z, 2, LW, TN), f32),
-            pltpu.VMEM((NB, Z, LW, TN), bf),
-            pltpu.VMEM((NB, Z, LW, TN), bf),
-            pltpu.VMEM((NB, Z, LW, TN), f32),
-            pltpu.VMEM((NB, Z - 1, LW, TN), bf),
-            pltpu.VMEM((NB, Z - 1, LW, TN), bf),
+            pltpu.VMEM((Z, 2, HL, TN), f32),
+            pltpu.VMEM((2 * NB, Z, HL, TN), bf),
+            pltpu.VMEM((2 * NB, Z, HL, TN), bf),
+            pltpu.VMEM((2 * NB, Z, HL, TN), f32),
+            pltpu.VMEM((2 * NB, Z - 1, HL, TN), bf),
+            pltpu.VMEM((2 * NB, Z - 1, HL, TN), bf),
             pltpu.VMEM((V, 8, 128), f32),
             dma((BUFS,)), dma((2,)), dma(()),
-            dma((NK, Z - 1)), dma((NK, Z - 1)), dma((NK, Z)), dma((NK, Z)),
-            dma((NC,)), dma((NC,)), dma((NC, X - 1)), dma((NC, X - 1)),
-            dma((NC, X - 1)), dma((NC, X - 1)), dma((NC, X)), dma((NC, X)),
-            dma((NB,)), dma((NB,)), dma((NB, Z - 1)), dma((NB, Z - 1)),
+            dma((2 * NK, Z - 1)), dma((2 * NK, Z - 1)), dma((2 * NK, Z)), dma((2 * NK, Z)),
+            dma((2 * NC,)), dma((2 * NC,)), dma((2 * NC, X - 1)), dma((2 * NC, X - 1)),
+            dma((2 * NC, X - 1)), dma((2 * NC, X - 1)), dma((2 * NC, X)), dma((2 * NC, X)),
+            dma((2 * NB,)), dma((2 * NB,)), dma((2 * NB, Z - 1)), dma((2 * NB, Z - 1)),
             dma((V - 1,)), dma((V - 1,)),
         ],
         compiler_params=pltpu.CompilerParams(
             collective_id=0, has_side_effects=True, vmem_limit_bytes=56 * 1024 * 1024
         ),
         name="walker_step",
-    )(green, chol, fields)
+    )(green, chol, fields.reshape(V, 2, HL, C))
     return potential, weight[0, :S] / (C * V)
 
 

time: 157 us -> 138 us (0.88)
  Pallas kernels: 152 us -> 134 us
    pallas_call x1, Pallas kernels: 152 us -> 134 us  [shards(): pl.pallas_call(functools.partial(kernel, dims), out_shape=(jax.ShapeDtype...]
where the time goes in v2:
time: 138 us
  Pallas kernels  134 us (97%)
  local copies, waits for them, and re-layouts  2.26 us (2%)
    pallas_call x1, Pallas kernels, shards(): pl.pallas_call(functools.partial(kernel, dims), out_shape=(jax.ShapeDtype...  134 us

profile of v2, /device:TPU:0, one launch (start us, length us, event | category | flops | bytes accessed | tf_op | source)
XLA Modules:
  0.0 137.7 jit_solution(997760530057291776)
XLA Ops:
  0.6 133.6 %walker_step.1 = (f32[32,8192]{1,0:T(8,128)}, f32[8,128]{1,0:T(8,128)}) custom-call(bf16[32,8192]{1,0:T(8,128)(2,1)} %green_ref.1, bf16[3072,8192]{1,0:T(8,128)(2,1)} %chol_ref.1, bf16[8,2,16,3072]{3,2,1,0:T(8,128)(2,1)} %bitcast.3), custom_call_target="tpu_custom_call" | custom-call | tf_op jit(solution)/shard_map/walker_step/pallas_call | solution.py:334
  134.3 1.2 multiply_bitcast_fusion
  135.5 2.3 %copy.6 = f32[32,8192]{1,0:T(8,128)} copy(f32[32,8192]{1,0:T(8,128)} %get-tuple-element.8) | data formatting | bytes 2097152
